TPU v7x, 128 devices: a whole 4x4x4 slice. The times are simulated.
128 devices in a mesh: row: 8 (over x_hi, z), col: 16 (over x_lo, y, core).
Axes of the slice: x: 4 (x_hi: 2, x_lo: 2; x = x_hi * 2 + x_lo), y: 4, z: 4, core: 2. Of those that a mesh axis runs over, the one named last changes fastest.
Arguments:
- left: float32 [2, 8192, 2560], P(None, 'row', 'col'), may hold values from -6 to 6
- right: float32 [2, 2560, 8192], P(None, 'row', 'col'), may hold values from -0.078125 to 0.078125
- prefix_owner: int32 [64], replicated, may hold values from 0 to 63, each once
- qubit_order: int32 [7], replicated, may hold values from 0 to 6, each once
Outputs:
- relaid: float32 [2, 8192, 8192], P(None, ('row', 'col'))
Inputs may be any that keep to these rules, and one draw needn't show every extreme that they name: `prefix_owner`: each prefix has exactly one owner, each owner one prefix. `qubit_order`: each open qubit appears once.
All inputs are finite; a program needn't handle non-finite values.
Results may differ from a plain program's by a relative error of at most 0.00007.
Values sent between devices are 32-bit elements; how exact they have to be, the bound alone decides.
A program may use at most 192 MiB of HBM per device.

v0:
```python
import jax
import jax.numpy as jnp
import numpy as np
from jax import lax
from jax.sharding import Mesh
from jax.sharding import PartitionSpec as P

LOW_BITS = 7
PREFIXES = 64
ROW = ("xh", "z")
CHIPS = ("xl", "y")
CORE = "core"
COL = ("xl", "y", "core")


def inverse_owner(prefix_owner, prefixes):
    labels = jnp.arange(prefixes, dtype=jnp.int32)
    match = (prefix_owner[None, :] == labels[:, None]).astype(jnp.int32)
    return jnp.sum(match * labels[None, :], axis=1)


def inner_order(qubit_order, low_bits):
    span = 2**low_bits
    offset = jnp.arange(span, dtype=jnp.int32)
    bits = jnp.bitwise_and(jnp.right_shift(offset[:, None], qubit_order[None, :]), 1)
    powers = jnp.left_shift(jnp.ones((low_bits,), jnp.int32), jnp.arange(low_bits, dtype=jnp.int32))
    return jnp.sum(bits * powers[None, :], axis=1)


def permute_left(left, prefix_owner, qubit_order, row_count, col_count):
    _, rows, kcols = left.shape
    span = 2**LOW_BITS
    local = rows // span
    sub = span // row_count
    x = left.reshape(2, local, row_count, sub, kcols)
    x = lax.all_to_all(x, ROW, split_axis=2, concat_axis=2, tiled=True)
    x = x.reshape(2, local * row_count, sub, kcols)
    inv = inverse_owner(prefix_owner, PREFIXES)
    pick = inv % local * row_count + inv // local
    y = jnp.take(x, pick, axis=1)
    y = y.reshape(2, row_count, local, sub, kcols)
    y = lax.all_to_all(y, ROW, split_axis=1, concat_axis=1, tiled=True)
    y = y.reshape(2, row_count * local * sub, kcols)
    s = inner_order(qubit_order, LOW_BITS)
    o_local = jnp.arange(local, dtype=jnp.int32)
    idx = s[None, :] // sub * (local * sub) + o_local[:, None] * sub + s[None, :] % sub
    idx = idx.reshape(-1)
    return jnp.take(y, jnp.take(idx, part_order(rows, col_count)), axis=1)


def part_sizes(q_total):
    return [q_total * 3 // 4, q_total - q_total * 3 // 4]


def part_order(rows, col_count):
    q_total = rows // col_count
    pos = []
    off = 0
    for qp in part_sizes(q_total):
        for c in range(col_count):
            pos.extend((c * q_total + off + i for i in range(qp)))
        off += qp
    return np.asarray(pos, np.int32)


def body(left, right, prefix_owner, qubit_order):
    row_count = lax.axis_size(ROW)
    col_count = lax.axis_size(COL)
    rows = left.shape[1]
    cols = right.shape[2]
    rpiece = jnp.swapaxes(right, 0, 1).reshape(right.shape[1], 2 * cols)
    rall = lax.all_gather(rpiece, ROW, axis=0, tiled=True)
    lp = permute_left(left, prefix_owner, qubit_order, row_count, col_count)
    lt = jnp.swapaxes(lp, 1, 2)
    lt = lax.optimization_barrier((lt, rall))[0]
    high = lax.Precision.HIGH
    dims = (((0,), (0,)), ((), ()))
    dot = lambda a, b: lax.dot_general(
        a, b, dims, preferred_element_type=jnp.float32, precision=high
    )
    outs = []
    prev = None
    start = 0
    for qp in part_sizes(rows // col_count):
        part = qp * col_count
        piece = lt[:, :, start : start + part]
        start += part
        piece = jnp.swapaxes(piece, 0, 1).reshape(piece.shape[1], 2 * part)
        if prev is not None:
            piece = lax.optimization_barrier((piece, prev))[0]
        lall = lax.all_gather(piece, COL, axis=0, tiled=True)
        prev = lall
        q = dot(lall, rall)
        re = q[:part, :cols] - q[part:, cols:]
        im = q[:part, cols:] + q[part:, :cols]
        tile = jnp.stack([re, im], axis=0)
        tile = tile.reshape(2, col_count, qp, cols)
        outs.append(lax.all_to_all(tile, COL, split_axis=1, concat_axis=3, tiled=True))
    out = jnp.concatenate(outs, axis=2)
    return out.reshape(2, rows // col_count, col_count * cols)


def solution(mesh):
    devices = np.asarray(mesh.devices)
    nr, nc = devices.shape
    fine = Mesh(devices.reshape(2, nr // 2, 2, nc // 4, 2), ("xh", "z", "xl", "y", "core"))
    in_specs = (P(None, ROW, COL), P(None, ROW, COL), P(), P())
    out_specs = P(None, ROW + COL, None)
    return jax.shard_map(body, mesh=fine, in_specs=in_specs, out_specs=out_specs, check_vma=False)
```

profile of v0, /device:TPU:1, one launch (start us, length us, event | category | flops | bytes accessed | tf_op | source)
XLA Modules:
  0.0 377.7 jit_solution(4709633685626059220)
XLA Ops:
  6.5 2.6 copy.59
  9.2 0.8 copy.44
  10.0 1.6 copy.45
  11.6 8.5 %all-to-all-start = ((f32[2,8,8,16,160]{4,3,1,0,2:T(8,128)}), f32[2,8,8,16,160]{4,3,1,0,2:T(8,128)S(1)}, u32[]{:S(2)}, u32[]{:S(2)}) async-start(f32[2,8,8,16,160]{4,3,1,0,2:T(8,128)} %copy.45), calls=%async_computation | async-start | bytes 4194304 | tf_op jit(solution)/shard_map/all_to_all | solution.py:36
  20.4 39.1 %all-to-all-done = f32[2,8,8,16,160]{4,3,1,0,2:T(8,128)S(1)} async-done(((f32[2,8,8,16,160]{4,3,1,0,2:T(8,128)}), f32[2,8,8,16,160]{4,3,1,0,2:T(8,128)S(1)}, u32[]{:S(2)}, u32[]{:S(2)}) %all-to-all-start) | async-done | bytes 1310752 | tf_op jit(solution)/shard_map/all_to_all | solution.py:36
  59.5 1.6 copy.46
  61.1 2.3 gather_fusion.1
  63.4 1.5 copy_select_fusion
  64.9 4.1 %all-to-all-start.1 = ((f32[2,8,8,16,160]{4,3,2,0,1:T(8,128)}), f32[2,8,8,16,160]{4,3,2,0,1:T(8,128)S(1)}, u32[]{:S(2)}, u32[]{:S(2)}) async-start(f32[2,8,8,16,160]{4,3,2,0,1:T(8,128)} %copy_select_fusion), calls=%async_computation.1 | async-start | bytes 4194304 | tf_op jit(solution)/shard_map/all_to_all | solution.py:42
  69.2 4.5 %gather_fusion = s32[1024]{0:T(1024)S(1)} fusion(s32[1024]{0:T(1024)S(1)} %add_bitcast_fusion, s32[1024]{0:T(1024)S(1)} %broadcast_clamp_fusion), kind=kCustom, calls=%fused_computation | custom fusion | bytes 12288 | tf_op jit(solution)/shard_map/jit(_take)/gather | solution.py:48
  73.7 33.3 %all-to-all-done.1 = f32[2,8,8,16,160]{4,3,2,0,1:T(8,128)S(1)} async-done(((f32[2,8,8,16,160]{4,3,2,0,1:T(8,128)}), f32[2,8,8,16,160]{4,3,2,0,1:T(8,128)S(1)}, u32[]{:S(2)}, u32[]{:S(2)}) %all-to-all-start.1) | async-done | bytes 1310752 | tf_op jit(solution)/shard_map/all_to_all | solution.py:42
  107.2 2.9 copy.49
  110.1 5.8 %gather_fusion.2 = f32[1024,2,160]{2,1,0:T(2,128)S(1)} fusion(f32[2,1024,160]{2,0,1:T(2,128)} %copy.49, s32[1024]{0:T(1024)S(1)} %fusion.6), kind=kCustom, calls=%fused_computation.2 | custom fusion | bytes 2625536 | tf_op jit(solution)/shard_map/jit(_take)/gather | solution.py:48
  115.9 4.5 %select_bitcast_fusion = f32[2,160,1024]{1,0,2:T(2,128)} fusion(f32[1024,2,160]{2,1,0:T(2,128)S(1)} %gather_fusion.2, pred[1024]{0:T(1024)(128)(4,1)S(1)} %compare_and_fusion.1), kind=kLoop, calls=%fused_computation.6 | loop fusion | flops 327680 | bytes 2622464 | tf_op jit(solution)/shard_map/jit(_take)/select_n | solution.py:48
  120.4 49.8 %all-gather.4.cloned.1.call-done = f32[2560,1024]{1,0:T(8,128)} async-done(((f32[320,1024]{1,0:T(8,128)}), f32[2560,1024]{1,0:T(8,128)}) %all-gather.4.cloned.1.call-update) | async-done | bytes 10485776 | tf_op jit(solution)/shard_map/all_gather | solution.py:72
  170.2 1.9 slice_bitcast_fusion
  172.1 1.8 copy.51
  173.9 1.0 copy.62
  175.2 1.2 slice_bitcast_fusion.1
  177.6 82.2 %all-gather.6.cloned.1.call-done = f32[2560,1536]{1,0:T(8,128)} async-done(((f32[160,1536]{1,0:T(8,128)}), f32[2560,1536]{1,0:T(8,128)}) %all-gather.6.cloned.1.call-update) | async-done | bytes 15728656 | tf_op jit(solution)/shard_map/all_gather | solution.py:91
  259.8 31.6 %fusion.11 = f32[1536,1024]{1,0:T(8,128)S(1)} fusion(f32[2560,1536]{1,0:T(8,128)} %all-gather.6.cloned.1.call-done, f32[2560,1024]{1,0:T(8,128)} %all-gather.4.cloned.1.call-done), kind=kOutput, calls=%fused_computation.55 | convolution fusion | flops 24159191040 | bytes 32505856 | tf_op jit(solution)/shard_map/dot_general | solution.py:78
  292.1 2.2 pad_maximum_fusion
  294.3 5.0 %all-to-all-start.2 = ((f32[2,16,48,512]{3,2,0,1:T(8,128)}), f32[2,16,48,512]{3,2,0,1:T(8,128)S(1)}, u32[]{:S(2)}, u32[]{:S(2)}) async-start(f32[2,16,48,512]{3,2,0,1:T(8,128)} %pad_maximum_fusion), calls=%async_computation.2 | async-start | bytes 6291456 | tf_op jit(solution)/shard_map/all_to_all | solution.py:98
  299.3 2.5 all-gather.8.cloned.1.call-done
  301.9 12.1 %fusion.12 = f32[512,1024]{1,0:T(8,128)S(1)} fusion(f32[2560,512]{1,0:T(8,128)} %all-gather.8.cloned.1.call-done, f32[2560,1024]{1,0:T(8,128)} %all-gather.4.cloned.1.call-done), kind=kOutput, calls=%fused_computation.56 | convolution fusion | flops 8053063680 | bytes 17825792 | tf_op jit(solution)/shard_map/dot_general | solution.py:78
  314.2 1.1 pad_maximum_fusion.1
  315.2 24.4 %all-to-all-done.2 = f32[2,16,48,512]{3,2,0,1:T(8,128)S(1)} async-done(((f32[2,16,48,512]{3,2,0,1:T(8,128)}), f32[2,16,48,512]{3,2,0,1:T(8,128)S(1)}, u32[]{:S(2)}, u32[]{:S(2)}) %all-to-all-start.2) | async-done | bytes 3145760 | tf_op jit(solution)/shard_map/all_to_all | solution.py:98
  339.7 10.1 %all-to-all-start.3 = ((f32[2,16,16,512]{3,2,0,1:T(8,128)}), f32[2,16,16,512]{3,2,0,1:T(8,128)}, u32[]{:S(2)}, u32[]{:S(2)}) async-start(f32[2,16,16,512]{3,2,0,1:T(8,128)} %pad_maximum_fusion.1), calls=%async_computation.3 | async-start | bytes 2097152 | tf_op jit(solution)/shard_map/all_to_all | solution.py:98
  349.7 2.1 copy.60
  351.8 13.8 %all-to-all-done.3 = f32[2,16,16,512]{3,2,0,1:T(8,128)} async-done(((f32[2,16,16,512]{3,2,0,1:T(8,128)}), f32[2,16,16,512]{3,2,0,1:T(8,128)}, u32[]{:S(2)}, u32[]{:S(2)}) %all-to-all-start.3) | async-done | bytes 1048608 | tf_op jit(solution)/shard_map/all_to_all | solution.py:98
  365.7 1.3 copy.61
  367.0 4.2 %maximum_bitcast_fusion = f32[2,64,8192]{2,1,0:T(8,128)} fusion(f32[2,1,16,8192]{3,2,0,1:T(8,128)S(1)} %bitcast.75, f32[2,1,48,8192]{3,2,0,1:T(8,128)} %bitcast.67), kind=kLoop, calls=%fused_computation.3 | loop fusion | flops 1048576 | bytes 8388608 | tf_op jit(solution)/shard_map/reshape | solution.py:100
  (32 shorter events, 3.1 us)
Async XLA Ops:
  6.5 2.7 copy-start
  6.5 163.6 %all-gather.4.cloned.1.call-start = ((), (), s32[]{:S(2)}) async-start(), calls=%async_computation.4 | async-start | bytes 11796480 | tf_op jit(solution)/shard_map/all_gather | solution.py:72
  11.6 8.5 %copy-start.2 = (s32[64]{0:T(128)S(1)}, s32[64]{0:T(128)}, u32[]{:S(2)}) copy-start(s32[64]{0:T(128)} %param.7) | copy-start | bytes 772
  11.6 8.7 %copy-start.3 = (s32[7]{0:T(128)S(1)}, s32[7]{0:T(128)}, u32[]{:S(2)}) copy-start(s32[7]{0:T(128)} %param.8) | copy-start | bytes 88
  11.6 47.9 %all-to-all-start = ((f32[2,8,8,16,160]{4,3,1,0,2:T(8,128)}), f32[2,8,8,16,160]{4,3,1,0,2:T(8,128)S(1)}, u32[]{:S(2)}, u32[]{:S(2)}) async-start(f32[2,8,8,16,160]{4,3,1,0,2:T(8,128)} %copy.45), calls=%async_computation | async-start | bytes 4194304 | tf_op jit(solution)/shard_map/all_to_all | solution.py:36
  64.9 4.3 %copy-start.1 = (s32[1024]{0:T(1024)S(1)}, s32[1024]{0:T(1024)}, u32[]{:S(2)}) copy-start(s32[1024]{0:T(1024)} %constant.116) | copy-start | bytes 12292
  64.9 42.1 %all-to-all-start.1 = ((f32[2,8,8,16,160]{4,3,2,0,1:T(8,128)}), f32[2,8,8,16,160]{4,3,2,0,1:T(8,128)S(1)}, u32[]{:S(2)}, u32[]{:S(2)}) async-start(f32[2,8,8,16,160]{4,3,2,0,1:T(8,128)} %copy_select_fusion), calls=%async_computation.1 | async-start | bytes 4194304 | tf_op jit(solution)/shard_map/all_to_all | solution.py:42
  69.0 190.8 %all-gather.6.cloned.1.call-start = ((), (), s32[]{:S(2)}) async-start(), calls=%async_computation.5 | async-start | bytes 16711680 | tf_op jit(solution)/shard_map/all_gather | solution.py:91
  174.9 126.9 %all-gather.8.cloned.1.call-start = ((), (), s32[]{:S(2)}) async-start(), calls=%async_computation.6 | async-start | bytes 5570560 | tf_op jit(solution)/shard_map/all_gather | solution.py:91
  294.3 45.3 %all-to-all-start.2 = ((f32[2,16,48,512]{3,2,0,1:T(8,128)}), f32[2,16,48,512]{3,2,0,1:T(8,128)S(1)}, u32[]{:S(2)}, u32[]{:S(2)}) async-start(f32[2,16,48,512]{3,2,0,1:T(8,128)} %pad_maximum_fusion), calls=%async_computation.2 | async-start | bytes 6291456 | tf_op jit(solution)/shard_map/all_to_all | solution.py:98
  339.7 26.0 %all-to-all-start.3 = ((f32[2,16,16,512]{3,2,0,1:T(8,128)}), f32[2,16,16,512]{3,2,0,1:T(8,128)}, u32[]{:S(2)}, u32[]{:S(2)}) async-start(f32[2,16,16,512]{3,2,0,1:T(8,128)} %pad_maximum_fusion.1), calls=%async_computation.3 | async-start | bytes 2097152 | tf_op jit(solution)/shard_map/all_to_all | solution.py:98
Sparse Core Ops, SparseCore 0:
  9.7 160.4 all-gather.3
  175.1 84.6 all-gather.5
  261.5 40.3 all-gather.7
where the time goes:
time: 378 us
  waiting for transfers between devices  245 us (65%)
  matrix products  43.7 us (12%)
  local copies, waits for them, and re-layouts  32.8 us (9%)
  starting transfers between devices  27.9 us (7%)
  other arithmetic  14.7 us (4%)
  between operations  13.3 us (4%)
    all_gather x2, waiting for transfers between devices, body(): lall = lax.all_gather(piece, COL, axis=0, tiled=True)  84.7 us
    all_gather x1, waiting for transfers between devices, body(): rall = lax.all_gather(rpiece, ROW, axis=0, tiled=True)  49.8 us
    dot_general x2, matrix products, body(): lax.dot_general(a, b, dims, preferred_element_type=jnp.float32, precision...  43.7 us
    all_to_all x1, waiting for transfers between devices, permute_left(): x = lax.all_to_all(x, ROW, split_axis=2, concat_axis=2, tiled=True)  39.1 us
    all_to_all x2, waiting for transfers between devices, body(): lax.all_to_all(tile, COL, split_axis=1, concat_axis=3, tiled=True)  38.3 us
    all_to_all x1, waiting for transfers between devices, permute_left(): y = lax.all_to_all(y, ROW, split_axis=1, concat_axis=1, tiled=True)  33.3 us
    all_to_all x2, starting transfers between devices, body(): lax.all_to_all(tile, COL, split_axis=1, concat_axis=3, tiled=True)  15.1 us
    gather x2, local copies, waits for them, and re-layouts, permute_left(): return jnp.take(y, jnp.take(idx, part_order(rows, col_count)), axis=1)  10.3 us
  transfers between devices with their start and end apart: 7, of which 7 were waited for; matrix products, arithmetic and copies ran while one was open for 21% of the time, Pallas kernels for 0%

commit v1 on v0

--- a/solution.py
+++ b/solution.py
@@ -69,7 +69,10 @@
     rows = left.shape[1]
     cols = right.shape[2]
     rpiece = jnp.swapaxes(right, 0, 1).reshape(right.shape[1], 2 * cols)
-    rall = lax.all_gather(rpiece, ROW, axis=0, tiled=True)
+    try_all_groups_by_axis = lambda raw, ax_name: jnp.concatenate(
+        lax.all_to_all(jnp.stack([raw for _ in range(lax.psum(1, ax_name))]), ax_name, 0, 0), axis=0
+    )
+    rall = try_all_groups_by_axis(rpiece, ROW)
     lp = permute_left(left, prefix_owner, qubit_order, row_count, col_count)
     lt = jnp.swapaxes(lp, 1, 2)
     lt = lax.optimization_barrier((lt, rall))[0]

time: 378 us -> 419 us (1.11)
  waiting for transfers between devices: 245 us -> 274 us
  starting transfers between devices: 27.9 us -> 34.3 us
  local copies, waits for them, and re-layouts: 32.8 us -> 37.9 us
    all_to_all x0 -> x1, waiting for transfers between devices: none -> 98 us  [body(): lax.all_to_all(jnp.stack([raw for _ in range(lax.psum(1, ax_name))]), ax_...]
    all_gather x1 -> x0, waiting for transfers between devices: 49.8 us -> none  [body(): rall = lax.all_gather(rpiece, ROW, axis=0, tiled=True)]
    all_to_all x1, waiting for transfers between devices: 39.1 us -> 25.9 us  [permute_left(): x = lax.all_to_all(x, ROW, split_axis=2, concat_axis=2, tiled=True)]
    all_to_all x1, waiting for transfers between devices: 33.3 us -> 24.7 us  [permute_left(): y = lax.all_to_all(y, ROW, split_axis=1, concat_axis=1, tiled=True)]
    another operation x0 -> x2, local copies, waits for them, and re-layouts: none -> 6.74 us  [body(): jnp.stack([raw for _ in range(lax.psum(1, ax_name))])]
    all_to_all x0 -> x1, starting transfers between devices: none -> 5.32 us  [body(): lax.all_to_all(jnp.stack([raw for _ in range(lax.psum(1, ax_name))]), ax_...]
  transfers between devices with their start and end apart: 7 -> 7, of which waited for: 7 -> 7; matrix products, arithmetic and copies ran while one was open for 21% -> 17% of each run, Pallas kernels for 0% -> 0%
where the time goes in v1:
time: 419 us; the launch traced here: 418 us
  waiting for transfers between devices  274 us (65%)
  matrix products  43.7 us (10%)
  local copies, waits for them, and re-layouts  37.9 us (9%)
  starting transfers between devices  34.3 us (8%)
  other arithmetic  14.7 us (4%)
  between operations  13.6 us (3%)
    all_to_all x1, waiting for transfers between devices, body(): lax.all_to_all(jnp.stack([raw for _ in range(lax.psum(1, ax_name))]), ax_...  98 us
    all_gather x2, waiting for transfers between devices, body(): lall = lax.all_gather(piece, COL, axis=0, tiled=True)  87.2 us
    dot_general x2, matrix products, body(): lax.dot_general(a, b, dims, preferred_element_type=jnp.float32, precision...  43.7 us
    all_to_all x2, waiting for transfers between devices, body(): lax.all_to_all(tile, COL, split_axis=1, concat_axis=3, tiled=True)  38.1 us
    all_to_all x1, waiting for transfers between devices, permute_left(): x = lax.all_to_all(x, ROW, split_axis=2, concat_axis=2, tiled=True)  25.9 us
    all_to_all x1, waiting for transfers between devices, permute_left(): y = lax.all_to_all(y, ROW, split_axis=1, concat_axis=1, tiled=True)  24.7 us
    all_to_all x2, starting transfers between devices, body(): lax.all_to_all(tile, COL, split_axis=1, concat_axis=3, tiled=True)  15.1 us
    gather x2, local copies, waits for them, and re-layouts, permute_left(): return jnp.take(y, jnp.take(idx, part_order(rows, col_count)), axis=1)  10.3 us
  transfers between devices with their start and end apart: 7, of which 7 were waited for; matrix products, arithmetic and copies ran while one was open for 17% of the time, Pallas kernels for 0%

profile of v1, /device:TPU:1, one launch (start us, length us, event | category | flops | bytes accessed | tf_op | source)
XLA Modules:
  0.0 418.2 jit_solution(9482001177819649438)
XLA Ops:
  6.5 1.8 copy.44
  8.3 1.6 copy.45
  9.9 8.5 %all-to-all-start = ((f32[2,8,8,16,160]{4,3,1,0,2:T(8,128)}), f32[2,8,8,16,160]{4,3,1,0,2:T(8,128)S(1)}, u32[]{:S(2)}, u32[]{:S(2)}) async-start(f32[2,8,8,16,160]{4,3,1,0,2:T(8,128)} %copy.45), calls=%async_computation | async-start | bytes 4194304 | tf_op jit(solution)/shard_map/all_to_all | solution.py:36
  18.6 25.9 %all-to-all-done = f32[2,8,8,16,160]{4,3,1,0,2:T(8,128)S(1)} async-done(((f32[2,8,8,16,160]{4,3,1,0,2:T(8,128)}), f32[2,8,8,16,160]{4,3,1,0,2:T(8,128)S(1)}, u32[]{:S(2)}, u32[]{:S(2)}) %all-to-all-start) | async-done | bytes 1310752 | tf_op jit(solution)/shard_map/all_to_all | solution.py:36
  44.5 1.6 copy.46
  46.0 2.3 gather_fusion.1
  48.3 1.5 copy_select_fusion
  49.9 5.2 %all-to-all-start.1 = ((f32[2,8,8,16,160]{4,3,2,0,1:T(8,128)}), f32[2,8,8,16,160]{4,3,2,0,1:T(8,128)S(1)}, u32[]{:S(2)}, u32[]{:S(2)}) async-start(f32[2,8,8,16,160]{4,3,2,0,1:T(8,128)} %copy_select_fusion), calls=%async_computation.1 | async-start | bytes 4194304 | tf_op jit(solution)/shard_map/all_to_all | solution.py:42
  55.1 1.4 copy.59
  56.5 24.7 %all-to-all-done.1 = f32[2,8,8,16,160]{4,3,2,0,1:T(8,128)S(1)} async-done(((f32[2,8,8,16,160]{4,3,2,0,1:T(8,128)}), f32[2,8,8,16,160]{4,3,2,0,1:T(8,128)S(1)}, u32[]{:S(2)}, u32[]{:S(2)}) %all-to-all-start.1) | async-done | bytes 1310752 | tf_op jit(solution)/shard_map/all_to_all | solution.py:42
  81.2 5.3 %stack.21 = f32[8,320,1024]{2,1,0:T(8,128)} broadcast(f32[320,1024]{1,0:T(8,128)S(1)} %bitcast.75), dimensions={1,2} | broadcast | bytes 11796480 | tf_op jit(solution)/shard_map/stack | solution.py:73
  86.5 5.3 %all-to-all-start.2 = ((f32[8,320,1024]{2,1,0:T(8,128)}), f32[8,320,1024]{2,1,0:T(8,128)}, u32[]{:S(2)}, u32[]{:S(2)}) async-start(f32[8,320,1024]{2,1,0:T(8,128)} %stack.21), calls=%async_computation.2 | async-start | bytes 20971520 | tf_op jit(solution)/shard_map/all_to_all | solution.py:73
  92.1 4.5 %gather_fusion = s32[1024]{0:T(1024)S(1)} fusion(s32[1024]{0:T(1024)S(1)} %add_bitcast_fusion, s32[1024]{0:T(1024)S(1)} %broadcast_clamp_fusion), kind=kCustom, calls=%fused_computation | custom fusion | bytes 12288 | tf_op jit(solution)/shard_map/jit(_take)/gather | solution.py:48
  96.9 2.9 copy.49
  99.8 5.8 %gather_fusion.2 = f32[1024,2,160]{2,1,0:T(2,128)S(1)} fusion(f32[2,1024,160]{2,0,1:T(2,128)} %copy.49, s32[1024]{0:T(1024)S(1)} %fusion.6), kind=kCustom, calls=%fused_computation.2 | custom fusion | bytes 2625536 | tf_op jit(solution)/shard_map/jit(_take)/gather | solution.py:48
  105.6 4.5 %select_bitcast_fusion = f32[2,160,1024]{1,0,2:T(2,128)} fusion(f32[1024,2,160]{2,1,0:T(2,128)S(1)} %gather_fusion.2, pred[1024]{0:T(1024)(128)(4,1)S(1)} %compare_and_fusion.1), kind=kLoop, calls=%fused_computation.6 | loop fusion | flops 327680 | bytes 2622464 | tf_op jit(solution)/shard_map/jit(_take)/select_n | solution.py:48
  110.0 98.0 %all-to-all-done.2 = f32[8,320,1024]{2,1,0:T(8,128)} async-done(((f32[8,320,1024]{2,1,0:T(8,128)}), f32[8,320,1024]{2,1,0:T(8,128)}, u32[]{:S(2)}, u32[]{:S(2)}) %all-to-all-start.2) | async-done | bytes 10485792 | tf_op jit(solution)/shard_map/all_to_all | solution.py:73
  208.0 1.9 slice_bitcast_fusion
  209.9 1.8 copy.51
  213.0 1.2 slice_bitcast_fusion.1
  215.4 84.5 %all-gather.3.cloned.1.call-done = f32[2560,1536]{1,0:T(8,128)} async-done(((f32[160,1536]{1,0:T(8,128)}), f32[2560,1536]{1,0:T(8,128)}) %all-gather.3.cloned.1.call-update) | async-done | bytes 15728656 | tf_op jit(solution)/shard_map/all_gather | solution.py:94
  299.9 31.6 %fusion.11 = f32[1536,1024]{1,0:T(8,128)S(1)} fusion(f32[2560,1536]{1,0:T(8,128)} %all-gather.3.cloned.1.call-done, f32[2560,1024]{1,0:T(8,128)} %bitcast.10), kind=kOutput, calls=%fused_computation.55 | convolution fusion | flops 24159191040 | bytes 32505856 | tf_op jit(solution)/shard_map/dot_general | solution.py:81
  332.3 2.2 pad_maximum_fusion
  334.5 5.0 %all-to-all-start.3 = ((f32[2,16,48,512]{3,2,0,1:T(8,128)}), f32[2,16,48,512]{3,2,0,1:T(8,128)S(1)}, u32[]{:S(2)}, u32[]{:S(2)}) async-start(f32[2,16,48,512]{3,2,0,1:T(8,128)} %pad_maximum_fusion), calls=%async_computation.3 | async-start | bytes 6291456 | tf_op jit(solution)/shard_map/all_to_all | solution.py:101
  339.5 2.7 all-gather.5.cloned.1.call-done
  342.2 12.1 %fusion.12 = f32[512,1024]{1,0:T(8,128)S(1)} fusion(f32[2560,512]{1,0:T(8,128)} %all-gather.5.cloned.1.call-done, f32[2560,1024]{1,0:T(8,128)} %bitcast.10), kind=kOutput, calls=%fused_computation.56 | convolution fusion | flops 8053063680 | bytes 17825792 | tf_op jit(solution)/shard_map/dot_general | solution.py:81
  355.6 24.2 %all-to-all-done.3 = f32[2,16,48,512]{3,2,0,1:T(8,128)S(1)} async-done(((f32[2,16,48,512]{3,2,0,1:T(8,128)}), f32[2,16,48,512]{3,2,0,1:T(8,128)S(1)}, u32[]{:S(2)}, u32[]{:S(2)}) %all-to-all-start.3) | async-done | bytes 3145760 | tf_op jit(solution)/shard_map/all_to_all | solution.py:101
  379.8 10.1 %all-to-all-start.4 = ((f32[2,16,16,512]{3,2,0,1:T(8,128)}), f32[2,16,16,512]{3,2,0,1:T(8,128)}, u32[]{:S(2)}, u32[]{:S(2)}) async-start(f32[2,16,16,512]{3,2,0,1:T(8,128)} %pad_maximum_fusion.1), calls=%async_computation.4 | async-start | bytes 2097152 | tf_op jit(solution)/shard_map/all_to_all | solution.py:101
  389.9 2.1 copy.60
  392.0 13.8 %all-to-all-done.4 = f32[2,16,16,512]{3,2,0,1:T(8,128)} async-done(((f32[2,16,16,512]{3,2,0,1:T(8,128)}), f32[2,16,16,512]{3,2,0,1:T(8,128)}, u32[]{:S(2)}, u32[]{:S(2)}) %all-to-all-start.4) | async-done | bytes 1048608 | tf_op jit(solution)/shard_map/all_to_all | solution.py:101
  405.8 1.3 copy.61
  407.1 4.2 %maximum_bitcast_fusion = f32[2,64,8192]{2,1,0:T(8,128)} fusion(f32[2,1,16,8192]{3,2,0,1:T(8,128)S(1)} %bitcast.76, f32[2,1,48,8192]{3,2,0,1:T(8,128)} %bitcast.68), kind=kLoop, calls=%fused_computation.3 | loop fusion | flops 1048576 | bytes 8388608 | tf_op jit(solution)/shard_map/reshape | solution.py:103
  (30 shorter events, 5.1 us)
Async XLA Ops:
  9.9 8.5 %copy-start.1 = (s32[64]{0:T(128)S(1)}, s32[64]{0:T(128)}, u32[]{:S(2)}) copy-start(s32[64]{0:T(128)} %param.7) | copy-start | bytes 772
  9.9 34.6 %all-to-all-start = ((f32[2,8,8,16,160]{4,3,1,0,2:T(8,128)}), f32[2,8,8,16,160]{4,3,1,0,2:T(8,128)S(1)}, u32[]{:S(2)}, u32[]{:S(2)}) async-start(f32[2,8,8,16,160]{4,3,1,0,2:T(8,128)} %copy.45), calls=%async_computation | async-start | bytes 4194304 | tf_op jit(solution)/shard_map/all_to_all | solution.py:36
  49.9 31.4 %all-to-all-start.1 = ((f32[2,8,8,16,160]{4,3,2,0,1:T(8,128)}), f32[2,8,8,16,160]{4,3,2,0,1:T(8,128)S(1)}, u32[]{:S(2)}, u32[]{:S(2)}) async-start(f32[2,8,8,16,160]{4,3,2,0,1:T(8,128)} %copy_select_fusion), calls=%async_computation.1 | async-start | bytes 4194304 | tf_op jit(solution)/shard_map/all_to_all | solution.py:42
  86.5 5.4 %copy-start.2 = (s32[7]{0:T(128)S(1)}, s32[7]{0:T(128)}, u32[]{:S(2)}) copy-start(s32[7]{0:T(128)} %param.8) | copy-start | bytes 88
  86.5 5.6 %copy-start = (s32[1024]{0:T(1024)S(1)}, s32[1024]{0:T(1024)}, u32[]{:S(2)}) copy-start(s32[1024]{0:T(1024)} %constant.116) | copy-start | bytes 12292
  86.5 121.4 %all-to-all-start.2 = ((f32[8,320,1024]{2,1,0:T(8,128)}), f32[8,320,1024]{2,1,0:T(8,128)}, u32[]{:S(2)}, u32[]{:S(2)}) async-start(f32[8,320,1024]{2,1,0:T(8,128)} %stack.21), calls=%async_computation.2 | async-start | bytes 20971520 | tf_op jit(solution)/shard_map/all_to_all | solution.py:73
  91.9 208.0 %all-gather.3.cloned.1.call-start = ((), (), s32[]{:S(2)}) async-start(), calls=%async_computation.5 | async-start | bytes 16711680 | tf_op jit(solution)/shard_map/all_gather | solution.py:94
  212.7 129.4 %all-gather.5.cloned.1.call-start = ((), (), s32[]{:S(2)}) async-start(), calls=%async_computation.6 | async-start | bytes 5570560 | tf_op jit(solution)/shard_map/all_gather | solution.py:94
  334.5 45.3 %all-to-all-start.3 = ((f32[2,16,48,512]{3,2,0,1:T(8,128)}), f32[2,16,48,512]{3,2,0,1:T(8,128)S(1)}, u32[]{:S(2)}, u32[]{:S(2)}) async-start(f32[2,16,48,512]{3,2,0,1:T(8,128)} %pad_maximum_fusion), calls=%async_computation.3 | async-start | bytes 6291456 | tf_op jit(solution)/shard_map/all_to_all | solution.py:101
  379.8 26.0 %all-to-all-start.4 = ((f32[2,16,16,512]{3,2,0,1:T(8,128)}), f32[2,16,16,512]{3,2,0,1:T(8,128)}, u32[]{:S(2)}, u32[]{:S(2)}) async-start(f32[2,16,16,512]{3,2,0,1:T(8,128)} %pad_maximum_fusion.1), calls=%async_computation.4 | async-start | bytes 2097152 | tf_op jit(solution)/shard_map/all_to_all | solution.py:101
Sparse Core Ops, SparseCore 0:
  212.9 86.9 all-gather.2
  301.6 40.4 all-gather.4
